TPU v7x, 32 devices: a whole 2x2x4 slice. The times are simulated.
32 devices in a mesh: dp: 2 (over x), fsdp: 16 (over z, y, core).
Axes of the slice: x: 2, y: 2, z: 4, core: 2. Of those that a mesh axis runs over, the one named last changes fastest.
Arguments:
- tokens: bfloat16 [32768, 1024], P(('dp', 'fsdp')), may hold values from -6 to 6
- w_query: bfloat16 [1024, 1024], P(('dp', 'fsdp')), may hold values from -0.1875 to 0.1875
- w_key: bfloat16 [1024, 1024], P(('dp', 'fsdp')), may hold values from -0.1875 to 0.1875
- w_value: bfloat16 [1024, 1024], P(('dp', 'fsdp')), may hold values from -0.1875 to 0.1875
- w_gate: bfloat16 [1024, 1024], P(('dp', 'fsdp')), may hold values from -0.1875 to 0.1875
- w_out: bfloat16 [1024, 1024], P(('dp', 'fsdp')), may hold values from -0.375 to 0.375
- w_one: bfloat16 [1024, 2816], P(('dp', 'fsdp')), may hold values from -0.1875 to 0.1875
- w_two: bfloat16 [1024, 2816], P(('dp', 'fsdp')), may hold values from -0.1875 to 0.1875
- w_three: bfloat16 [2816, 1024], P(('dp', 'fsdp')), may hold values from -0.109375 to 0.109375
- cotangent: bfloat16 [32768, 1024], P(('dp', 'fsdp')), may hold values from -6 to 6
Outputs:
- output: bfloat16 [32768, 1024], P(('dp', 'fsdp'))
- grad_tokens: bfloat16 [32768, 1024], P(('dp', 'fsdp'))
- grad_query: float32 [1024, 1024], P(('dp', 'fsdp'))
- grad_key: float32 [1024, 1024], P(('dp', 'fsdp'))
- grad_value: float32 [1024, 1024], P(('dp', 'fsdp'))
- grad_gate: float32 [1024, 1024], P(('dp', 'fsdp'))
- grad_out: float32 [1024, 1024], P(('dp', 'fsdp'))
- grad_one: float32 [1024, 2816], P(('dp', 'fsdp'))
- grad_two: float32 [1024, 2816], P(('dp', 'fsdp'))
- grad_three: float32 [2816, 1024], P(('dp', 'fsdp'))
All inputs are finite; a program needn't handle non-finite values.
Results may differ from a plain program's by a relative error of at most 0.014.
Values may be sent and summed in bfloat16 or wider, within the bound.
A program may use at most 256 MiB of HBM per device.

v0:
```python
import jax
import jax.numpy as jnp
from jax import lax
from jax.sharding import PartitionSpec as P

HEADS = 16
HEAD = 64
BLOCK = 128
SEQ = 1024


EPS = 1e-06


def row_scale(value):
    return lax.rsqrt(jnp.mean(value * value, axis=-1, keepdims=True) + EPS)


def scale_back(value, scale, grad):
    return scale * grad - value * scale * scale * scale * jnp.mean(
        grad * value, axis=-1, keepdims=True
    )


def logistic(value):
    return 1.0 / (1.0 + jnp.exp(-value))


def swish_slope(value):
    sig = logistic(value)
    return sig * (1.0 + value * (1.0 - sig))


def matmul(left, right):
    return jnp.dot(left, right, preferred_element_type=jnp.float32)


def matmul_tr(left, right):
    return lax.dot_general(
        left, right, (((1,), (1,)), ((), ())), preferred_element_type=jnp.float32
    )


def weight_grad(left, right):
    return lax.dot_general(
        left, right, (((0,), (0,)), ((), ())), preferred_element_type=jnp.float32
    )


def to_blocks(value):
    return value.reshape(-1, SEQ // BLOCK, BLOCK, HEADS, HEAD)


def local(tokens, w_query, w_key, w_value, w_gate, w_out, w_one, w_two, w_three, cotangent):
    attn_w = (
        lax.all_gather(w_query, ("dp", "fsdp"), axis=0, tiled=True),
        lax.all_gather(w_key, ("dp", "fsdp"), axis=0, tiled=True),
        lax.all_gather(w_value, ("dp", "fsdp"), axis=0, tiled=True),
        lax.all_gather(w_gate, ("dp", "fsdp"), axis=0, tiled=True),
        lax.all_gather(w_out, ("dp", "fsdp"), axis=0, tiled=True),
    )
    ffn_w = (
        lax.all_gather(w_one, ("dp", "fsdp"), axis=0, tiled=True),
        lax.all_gather(w_two, ("dp", "fsdp"), axis=0, tiled=True),
        lax.all_gather(w_three, ("dp", "fsdp"), axis=0, tiled=True),
    )
    wq, wk, wv, wu, wo = attn_w
    w1, w2, w3 = ffn_w
    x = tokens.astype(jnp.float32)
    scale_one = row_scale(x)
    normed = (x * scale_one).astype(jnp.bfloat16)
    pre_q = matmul(normed, wq)
    pre_k = matmul(normed, wk)
    pre_v = matmul(normed, wv)
    pre_u = matmul(normed, wu)
    q_blocks = to_blocks((pre_q * logistic(pre_q)).astype(jnp.bfloat16))
    k_blocks = to_blocks((pre_k * logistic(pre_k)).astype(jnp.bfloat16))
    v_blocks = to_blocks(pre_v.astype(jnp.bfloat16))
    causal = jnp.tril(jnp.ones((BLOCK, BLOCK), jnp.float32))
    scores = (
        jnp.einsum("bnchd,bnehd->bnhce", q_blocks, k_blocks, preferred_element_type=jnp.float32)
        * causal
    ).astype(jnp.bfloat16)
    inner = jnp.einsum("bnhce,bnehd->bnchd", scores, v_blocks, preferred_element_type=jnp.float32)
    block_kv = jnp.einsum(
        "bnchd,bnche->bnhde", k_blocks, v_blocks, preferred_element_type=jnp.float32
    )
    state = (jnp.cumsum(block_kv, axis=1) - block_kv).astype(jnp.bfloat16)
    outer = jnp.einsum("bnchd,bnhde->bnche", q_blocks, state, preferred_element_type=jnp.float32)
    attn = (inner + outer).reshape(x.shape)
    scale_two = row_scale(attn)
    attn_normed = attn * scale_two
    sig = logistic(pre_u)
    gated = (attn_normed * sig).astype(jnp.bfloat16)
    mid = x + matmul(gated, wo)
    scale_three = row_scale(mid)
    normed_two = (mid * scale_three).astype(jnp.bfloat16)
    first = matmul(normed_two, w1)
    second = matmul(normed_two, w2)
    product = (first * second).astype(jnp.bfloat16)
    output = (mid + matmul(product, w3)).astype(jnp.bfloat16)
    w1b, w2b, w3b = (
        lax.all_gather(w_one, ("dp", "fsdp"), axis=0, tiled=True),
        lax.all_gather(w_two, ("dp", "fsdp"), axis=0, tiled=True),
        lax.all_gather(w_three, ("dp", "fsdp"), axis=0, tiled=True),
    )
    grad_three = weight_grad(product, cotangent)
    dprod = matmul_tr(cotangent, w3b)
    d_first = (dprod * second).astype(jnp.bfloat16)
    d_second = (dprod * first).astype(jnp.bfloat16)
    grad_one = weight_grad(normed_two, d_first)
    grad_two = weight_grad(normed_two, d_second)
    d_normed_two = matmul_tr(d_first, w1b) + matmul_tr(d_second, w2b)
    d_mid = cotangent.astype(jnp.float32) + scale_back(mid, scale_three, d_normed_two)
    wqb, wkb, wvb, wub, wob = (
        lax.all_gather(w_query, ("dp", "fsdp"), axis=0, tiled=True),
        lax.all_gather(w_key, ("dp", "fsdp"), axis=0, tiled=True),
        lax.all_gather(w_value, ("dp", "fsdp"), axis=0, tiled=True),
        lax.all_gather(w_gate, ("dp", "fsdp"), axis=0, tiled=True),
        lax.all_gather(w_out, ("dp", "fsdp"), axis=0, tiled=True),
    )
    d_branch = d_mid.astype(jnp.bfloat16)
    grad_out = weight_grad(gated, d_branch)
    d_gated = matmul_tr(d_branch, wob)
    d_pre_u = (d_gated * attn_normed * sig * (1.0 - sig)).astype(jnp.bfloat16)
    d_attn = scale_back(attn, scale_two, d_gated * sig).astype(jnp.bfloat16)
    d_blocks = to_blocks(d_attn)
    d_scores = (
        jnp.einsum("bnchd,bnehd->bnhce", d_blocks, v_blocks, preferred_element_type=jnp.float32)
        * causal
    ).astype(jnp.bfloat16)
    d_state = jnp.einsum(
        "bnchd,bnche->bnhde", q_blocks, d_blocks, preferred_element_type=jnp.float32
    )
    d_kv = (lax.cumsum(d_state, axis=1, reverse=True) - d_state).astype(jnp.bfloat16)
    dq_full = jnp.einsum(
        "bnhce,bnehd->bnchd", d_scores, k_blocks, preferred_element_type=jnp.float32
    ) + jnp.einsum("bnche,bnhde->bnchd", d_blocks, state, preferred_element_type=jnp.float32)
    dk_full = jnp.einsum(
        "bnhce,bnchd->bnehd", d_scores, q_blocks, preferred_element_type=jnp.float32
    ) + jnp.einsum("bnche,bnhde->bnchd", v_blocks, d_kv, preferred_element_type=jnp.float32)
    dv_full = jnp.einsum(
        "bnhce,bnchd->bnehd", scores, d_blocks, preferred_element_type=jnp.float32
    ) + jnp.einsum("bnchd,bnhde->bnche", k_blocks, d_kv, preferred_element_type=jnp.float32)
    d_query = (dq_full.reshape(x.shape) * swish_slope(pre_q)).astype(jnp.bfloat16)
    d_key = (dk_full.reshape(x.shape) * swish_slope(pre_k)).astype(jnp.bfloat16)
    d_value = dv_full.reshape(x.shape).astype(jnp.bfloat16)
    grad_query = weight_grad(normed, d_query)
    grad_key = weight_grad(normed, d_key)
    grad_value = weight_grad(normed, d_value)
    grad_gate = weight_grad(normed, d_pre_u)
    d_normed = (
        matmul_tr(d_query, wqb)
        + matmul_tr(d_key, wkb)
        + matmul_tr(d_value, wvb)
        + matmul_tr(d_pre_u, wub)
    )
    grad_tokens = (d_mid + scale_back(x, scale_one, d_normed)).astype(jnp.bfloat16)
    shares = (
        lax.psum_scatter(grad_query, ("dp", "fsdp"), scatter_dimension=0, tiled=True),
        lax.psum_scatter(grad_key, ("dp", "fsdp"), scatter_dimension=0, tiled=True),
        lax.psum_scatter(grad_value, ("dp", "fsdp"), scatter_dimension=0, tiled=True),
        lax.psum_scatter(grad_gate, ("dp", "fsdp"), scatter_dimension=0, tiled=True),
        lax.psum_scatter(grad_out, ("dp", "fsdp"), scatter_dimension=0, tiled=True),
        lax.psum_scatter(grad_one, ("dp", "fsdp"), scatter_dimension=0, tiled=True),
        lax.psum_scatter(grad_two, ("dp", "fsdp"), scatter_dimension=0, tiled=True),
        lax.psum_scatter(grad_three, ("dp", "fsdp"), scatter_dimension=0, tiled=True),
    )
    return (
        output,
        grad_tokens,
        shares[0],
        shares[1],
        shares[2],
        shares[3],
        shares[4],
        shares[5],
        shares[6],
        shares[7],
    )


def solution(mesh):
    in_specs = (
        P(("dp", "fsdp"), None),
        P(("dp", "fsdp"), None),
        P(("dp", "fsdp"), None),
        P(("dp", "fsdp"), None),
        P(("dp", "fsdp"), None),
        P(("dp", "fsdp"), None),
        P(("dp", "fsdp"), None),
        P(("dp", "fsdp"), None),
        P(("dp", "fsdp"), None),
        P(("dp", "fsdp"), None),
    )
    out_specs = (
        P(("dp", "fsdp"), None),
        P(("dp", "fsdp"), None),
        P(("dp", "fsdp"), None),
        P(("dp", "fsdp"), None),
        P(("dp", "fsdp"), None),
        P(("dp", "fsdp"), None),
        P(("dp", "fsdp"), None),
        P(("dp", "fsdp"), None),
        P(("dp", "fsdp"), None),
        P(("dp", "fsdp"), None),
    )
    return jax.shard_map(local, mesh=mesh, in_specs=in_specs, out_specs=out_specs, check_vma=False)
```

profile of v0, /device:TPU:0, one launch (start us, length us, event | category | flops | bytes accessed | tf_op | source)
XLA Modules:
  0.0 1791.4 jit_solution(3578899942503564222)
XLA Ops:
  20.2 49.6 %all-gather.11.cloned.1.call-done = bf16[1024,1024]{1,0:T(8,128)(2,1)} async-done(((bf16[32,1024]{1,0:T(8,128)(2,1)}), bf16[1024,1024]{1,0:T(8,128)(2,1)}) %all-gather.11.cloned.1.call-update) | async-done | bytes 2097168 | tf_op jit(solution)/shard_map/all_gather | solution.py:56
  88.4 39.5 %all-gather.13.cloned.1.call-done = bf16[1024,1024]{1,0:T(8,128)(2,1)} async-done(((bf16[32,1024]{1,0:T(8,128)(2,1)}), bf16[1024,1024]{1,0:T(8,128)(2,1)}) %all-gather.13.cloned.1.call-update) | async-done | bytes 2097168 | tf_op jit(solution)/shard_map/all_gather | solution.py:57
  148.1 37.8 %all-gather.9.cloned.1.call-done = bf16[1024,1024]{1,0:T(8,128)(2,1)} async-done(((bf16[32,1024]{1,0:T(8,128)(2,1)}), bf16[1024,1024]{1,0:T(8,128)(2,1)}) %all-gather.9.cloned.1.call-update) | async-done | bytes 2097168 | tf_op jit(solution)/shard_map/all_gather | solution.py:58
  232.7 11.1 all-gather.15.cloned.1.call-done
  252.9 48.7 %all-gather.17.cloned.1.call-done = bf16[1024,1024]{1,0:T(8,128)(2,1)} async-done(((bf16[32,1024]{1,0:T(8,128)(2,1)}), bf16[1024,1024]{1,0:T(8,128)(2,1)}) %all-gather.17.cloned.1.call-update) | async-done | bytes 2097168 | tf_op jit(solution)/shard_map/all_gather | solution.py:60
  310.9 59.6 %all-gather.19.cloned.1.call-done = bf16[1024,2816]{1,0:T(8,128)(2,1)} async-done(((bf16[32,2816]{1,0:T(8,128)(2,1)}), bf16[1024,2816]{1,0:T(8,128)(2,1)}) %all-gather.19.cloned.1.call-update) | async-done | bytes 5767184 | tf_op jit(solution)/shard_map/all_gather | solution.py:63
  370.6 11.9 fusion.36
  382.4 57.0 %all-gather.21.cloned.1.call-done = bf16[1024,2816]{1,0:T(8,128)(2,1)} async-done(((bf16[32,2816]{1,0:T(8,128)(2,1)}), bf16[1024,2816]{1,0:T(8,128)(2,1)}) %all-gather.21.cloned.1.call-update) | async-done | bytes 5767184 | tf_op jit(solution)/shard_map/all_gather | solution.py:64
  439.4 12.1 fusion.37
  451.5 56.8 %all-gather.23.cloned.1.call-done = bf16[2816,1024]{1,0:T(8,128)(2,1)} async-done(((bf16[88,1024]{1,0:T(8,128)(2,1)}), bf16[2816,1024]{1,0:T(8,128)(2,1)}) %all-gather.23.cloned.1.call-update) | async-done | bytes 5767184 | tf_op jit(solution)/shard_map/all_gather | solution.py:65
  508.3 18.1 %multiply_convert_fusion = (bf16[1024,2816]{1,0:T(8,128)(2,1)}, bf16[1024,2816]{1,0:T(8,128)(2,1)}, bf16[1024,2816]{1,0:T(8,128)(2,1)}) fusion(f32[1024,2816]{1,0:T(8,128)} %fusion.36, f32[1024,2816]{1,0:T(8,128)} %fusion.37, bf16[1024,1024]{1,0:T(8,128)(2,1)} %param.19, bf16[2816,1024]{1,0:T(8,128)(2,1)} %all-gather.23.cloned.1.call-done), kind=kOutput, calls=%fused_computation | convolution fusion | flops 5922881536 | bytes 48234496 | tf_op jit(solution)/shard_map/dot_general | solution.py:39
  526.4 10.0 fusion.38
  669.1 11.8 fusion.45
  681.0 11.9 fusion.46
  692.9 12.2 fusion.47
  724.1 10.8 add_convert_fusion.1
  737.5 12.0 reduce-scatter.11.cloned.1.call-done
  749.5 141.1 %reduce-scatter.17.cloned.1.call-done = f32[32,1024]{1,0:T(8,128)} async-done(((f32[1024,1024]{1,0:T(8,128)}), f32[32,1024]{1,0:T(8,128)}) %reduce-scatter.17.cloned.1.call-update) | async-done | bytes 131088 | tf_op jit(solution)/shard_map/reduce_scatter | solution.py:164
  890.6 141.5 %reduce-scatter.9.cloned.1.call-done = f32[32,1024]{1,0:T(8,128)} async-done(((f32[1024,1024]{1,0:T(8,128)}), f32[32,1024]{1,0:T(8,128)}) %reduce-scatter.9.cloned.1.call-update) | async-done | bytes 131088 | tf_op jit(solution)/shard_map/reduce_scatter | solution.py:160
  1032.0 141.2 %reduce-scatter.13.cloned.1.call-done = f32[32,1024]{1,0:T(8,128)} async-done(((f32[1024,1024]{1,0:T(8,128)}), f32[32,1024]{1,0:T(8,128)}) %reduce-scatter.13.cloned.1.call-update) | async-done | bytes 131088 | tf_op jit(solution)/shard_map/reduce_scatter | solution.py:162
  1173.3 141.2 %reduce-scatter.15.cloned.1.call-done = f32[32,1024]{1,0:T(8,128)} async-done(((f32[1024,1024]{1,0:T(8,128)}), f32[32,1024]{1,0:T(8,128)}) %reduce-scatter.15.cloned.1.call-update) | async-done | bytes 131088 | tf_op jit(solution)/shard_map/reduce_scatter | solution.py:163
  1314.4 154.9 %reduce-scatter.19.cloned.1.call-done = f32[32,2816]{1,0:T(8,128)} async-done(((f32[1024,2816]{1,0:T(8,128)}), f32[32,2816]{1,0:T(8,128)}) %reduce-scatter.19.cloned.1.call-update) | async-done | bytes 360464 | tf_op jit(solution)/shard_map/reduce_scatter | solution.py:165
  1469.4 157.3 %reduce-scatter.21.cloned.1.call-done = f32[32,2816]{1,0:T(8,128)} async-done(((f32[1024,2816]{1,0:T(8,128)}), f32[32,2816]{1,0:T(8,128)}) %reduce-scatter.21.cloned.1.call-update) | async-done | bytes 360464 | tf_op jit(solution)/shard_map/reduce_scatter | solution.py:166
  1626.6 157.8 %reduce-scatter.23.cloned.1.call-done = f32[88,1024]{1,0:T(8,128)} async-done(((f32[2816,1024]{1,0:T(8,128)}), f32[88,1024]{1,0:T(8,128)}) %reduce-scatter.23.cloned.1.call-update) | async-done | bytes 360464 | tf_op jit(solution)/shard_map/reduce_scatter | solution.py:167
  (163 shorter events, 270.6 us)
Async XLA Ops:
  7.2 62.7 %all-gather.11.cloned.1.call-start = ((), (), s32[]{:S(2)}) async-start(), calls=%async_computation.9 | async-start | bytes 2162688 | tf_op jit(solution)/shard_map/all_gather | solution.py:56
  7.9 120.0 %all-gather.13.cloned.1.call-start = ((), (), s32[]{:S(2)}) async-start(), calls=%async_computation.10 | async-start | bytes 2162688 | tf_op jit(solution)/shard_map/all_gather | solution.py:57
  8.7 177.3 %all-gather.9.cloned.1.call-start = ((), (), s32[]{:S(2)}) async-start(), calls=%async_computation.8 | async-start | bytes 2162688 | tf_op jit(solution)/shard_map/all_gather | solution.py:58
  9.4 234.4 %all-gather.15.cloned.1.call-start = ((), (), s32[]{:S(2)}) async-start(), calls=%async_computation.11 | async-start | bytes 2162688 | tf_op jit(solution)/shard_map/all_gather | solution.py:59
  10.0 291.7 %all-gather.17.cloned.1.call-start = ((), (), s32[]{:S(2)}) async-start(), calls=%async_computation.12 | async-start | bytes 2162688 | tf_op jit(solution)/shard_map/all_gather | solution.py:60
  10.6 360.0 %all-gather.19.cloned.1.call-start = ((), (), s32[]{:S(2)}) async-start(), calls=%async_computation.13 | async-start | bytes 5947392 | tf_op jit(solution)/shard_map/all_gather | solution.py:63
  11.1 428.3 %all-gather.21.cloned.1.call-start = ((), (), s32[]{:S(2)}) async-start(), calls=%async_computation.14 | async-start | bytes 5947392 | tf_op jit(solution)/shard_map/all_gather | solution.py:64
  11.9 496.4 %all-gather.23.cloned.1.call-start = ((), (), s32[]{:S(2)}) async-start(), calls=%async_computation.15 | async-start | bytes 5947392 | tf_op jit(solution)/shard_map/all_gather | solution.py:65
  12.6 736.9 %reduce-scatter.11.cloned.1.call-start = ((), (), s32[]{:S(2)}) async-start(), calls=%async_computation.17 | async-start | bytes 4325376 | tf_op jit(solution)/shard_map/reduce_scatter | solution.py:161
  15.5 61.5 %copy-start.8 = (bf16[1024,1024]{0,1:T(8,128)(2,1)}, bf16[1024,1024]{0,1:T(8,128)(2,1)S(1)}, u32[]{:S(2)}) copy-start(bf16[1024,1024]{0,1:T(8,128)(2,1)S(1)} %copy.49) | copy-start | bytes 6291460
  526.4 10.0 copy-start.20
  526.4 10.1 copy-start.23
  536.4 8.6 copy-start.24
  546.7 7.4 copy-start.12
  597.5 6.4 copy-start.9
  608.3 282.3 %reduce-scatter.17.cloned.1.call-start = ((), (), s32[]{:S(2)}) async-start(), calls=%async_computation.20 | async-start | bytes 4325376 | tf_op jit(solution)/shard_map/reduce_scatter | solution.py:164
  616.4 6.0 copy-start.1
  616.4 415.6 %reduce-scatter.9.cloned.1.call-start = ((), (), s32[]{:S(2)}) async-start(), calls=%async_computation.16 | async-start | bytes 4325376 | tf_op jit(solution)/shard_map/reduce_scatter | solution.py:160
  640.1 6.4 copy-start.10
  650.9 522.4 %reduce-scatter.13.cloned.1.call-start = ((), (), s32[]{:S(2)}) async-start(), calls=%async_computation.18 | async-start | bytes 4325376 | tf_op jit(solution)/shard_map/reduce_scatter | solution.py:162
  663.1 651.3 %reduce-scatter.15.cloned.1.call-start = ((), (), s32[]{:S(2)}) async-start(), calls=%async_computation.19 | async-start | bytes 4325376 | tf_op jit(solution)/shard_map/reduce_scatter | solution.py:163
  669.1 800.3 %reduce-scatter.19.cloned.1.call-start = ((), (), s32[]{:S(2)}) async-start(), calls=%async_computation.21 | async-start | bytes 11894784 | tf_op jit(solution)/shard_map/reduce_scatter | solution.py:165
  681.0 945.7 %reduce-scatter.21.cloned.1.call-start = ((), (), s32[]{:S(2)}) async-start(), calls=%async_computation.22 | async-start | bytes 11894784 | tf_op jit(solution)/shard_map/reduce_scatter | solution.py:166
  692.9 1091.5 %reduce-scatter.23.cloned.1.call-start = ((), (), s32[]{:S(2)}) async-start(), calls=%async_computation.23 | async-start | bytes 11894784 | tf_op jit(solution)/shard_map/reduce_scatter | solution.py:167
  (26 other events, 75.2 us)
Sparse Core Ops, SparseCore 0:
  10.8 58.9 all-gather.10
  72.7 55.0 all-gather.12
  130.8 55.1 all-gather.8
  188.6 55.1 all-gather.14
  246.5 55.0 all-gather.16
  304.4 66.1 all-gather.18
  373.4 65.9 all-gather.20
  442.3 65.9 all-gather.22
  608.4 141.0 reduce-scatter.10
  752.2 138.3 reduce-scatter.16
  893.4 138.5 reduce-scatter.8
  1034.7 138.4 reduce-scatter.12
  1176.1 138.2 reduce-scatter.14
  1317.2 152.1 reduce-scatter.18
  1472.1 154.4 reduce-scatter.20
  1629.4 155.0 reduce-scatter.22
where the time goes:
time: 1800 us; the launch traced here: 1790 us
  waiting for transfers between devices  1410 us (78%)
  matrix products  218 us (12%)
  local copies, waits for them, and re-layouts  123 us (7%)
  other arithmetic  22.1 us (1%)
    reduce_scatter x1, waiting for transfers between devices, local(): lax.psum_scatter(grad_three, ('dp', 'fsdp'), scatter_dimension=0, tiled=T...  158 us
    reduce_scatter x1, waiting for transfers between devices, local(): lax.psum_scatter(grad_two, ('dp', 'fsdp'), scatter_dimension=0, tiled=True)  157 us
    reduce_scatter x1, waiting for transfers between devices, local(): lax.psum_scatter(grad_one, ('dp', 'fsdp'), scatter_dimension=0, tiled=True)  155 us
    reduce_scatter x1, waiting for transfers between devices, local(): lax.psum_scatter(grad_query, ('dp', 'fsdp'), scatter_dimension=0, tiled=T...  141 us
    reduce_scatter x1, waiting for transfers between devices, local(): lax.psum_scatter(grad_value, ('dp', 'fsdp'), scatter_dimension=0, tiled=T...  141 us
    reduce_scatter x1, waiting for transfers between devices, local(): lax.psum_scatter(grad_gate, ('dp', 'fsdp'), scatter_dimension=0, tiled=True)  141 us
    reduce_scatter x1, waiting for transfers between devices, local(): lax.psum_scatter(grad_out, ('dp', 'fsdp'), scatter_dimension=0, tiled=True)  141 us
    dot_general x8, matrix products, matmul(): return jnp.dot(left, right, preferred_element_type=jnp.float32)  70.3 us
  transfers between devices with their start and end apart: 16, of which 16 were waited for; matrix products, arithmetic and copies ran while one was open for 14% of the time, Pallas kernels for 0%

commit v1 on v0

--- a/solution.py
+++ b/solution.py
@@ -52,20 +52,22 @@
 
 
 def local(tokens, w_query, w_key, w_value, w_gate, w_out, w_one, w_two, w_three, cotangent):
-    attn_w = (
-        lax.all_gather(w_query, ("dp", "fsdp"), axis=0, tiled=True),
-        lax.all_gather(w_key, ("dp", "fsdp"), axis=0, tiled=True),
-        lax.all_gather(w_value, ("dp", "fsdp"), axis=0, tiled=True),
-        lax.all_gather(w_gate, ("dp", "fsdp"), axis=0, tiled=True),
-        lax.all_gather(w_out, ("dp", "fsdp"), axis=0, tiled=True),
-    )
-    ffn_w = (
-        lax.all_gather(w_one, ("dp", "fsdp"), axis=0, tiled=True),
-        lax.all_gather(w_two, ("dp", "fsdp"), axis=0, tiled=True),
-        lax.all_gather(w_three, ("dp", "fsdp"), axis=0, tiled=True),
-    )
-    wq, wk, wv, wu, wo = attn_w
-    w1, w2, w3 = ffn_w
+    axes = ("dp", "fsdp")
+    rows, width = w_query.shape
+    hidden = w_one.shape[1]
+    attn_all = lax.all_gather(
+        jnp.concatenate((w_query, w_key, w_value, w_gate, w_out), axis=1), axes, axis=0, tiled=True
+    )
+    ffn_all = lax.all_gather(
+        jnp.concatenate((w_one, w_two, w_three.reshape(rows, hidden)), axis=1),
+        axes,
+        axis=0,
+        tiled=True,
+    )
+    wq, wk, wv, wu, wo = (attn_all[:, i * width : (i + 1) * width] for i in range(5))
+    w1 = ffn_all[:, :hidden]
+    w2 = ffn_all[:, hidden : 2 * hidden]
+    w3 = ffn_all[:, 2 * hidden :].reshape(hidden, width)
     x = tokens.astype(jnp.float32)
     scale_one = row_scale(x)
     normed = (x * scale_one).astype(jnp.bfloat16)
@@ -99,29 +101,17 @@
     second = matmul(normed_two, w2)
     product = (first * second).astype(jnp.bfloat16)
     output = (mid + matmul(product, w3)).astype(jnp.bfloat16)
-    w1b, w2b, w3b = (
-        lax.all_gather(w_one, ("dp", "fsdp"), axis=0, tiled=True),
-        lax.all_gather(w_two, ("dp", "fsdp"), axis=0, tiled=True),
-        lax.all_gather(w_three, ("dp", "fsdp"), axis=0, tiled=True),
-    )
     grad_three = weight_grad(product, cotangent)
-    dprod = matmul_tr(cotangent, w3b)
+    dprod = matmul_tr(cotangent, w3)
     d_first = (dprod * second).astype(jnp.bfloat16)
     d_second = (dprod * first).astype(jnp.bfloat16)
     grad_one = weight_grad(normed_two, d_first)
     grad_two = weight_grad(normed_two, d_second)
-    d_normed_two = matmul_tr(d_first, w1b) + matmul_tr(d_second, w2b)
+    d_normed_two = matmul_tr(d_first, w1) + matmul_tr(d_second, w2)
     d_mid = cotangent.astype(jnp.float32) + scale_back(mid, scale_three, d_normed_two)
-    wqb, wkb, wvb, wub, wob = (
-        lax.all_gather(w_query, ("dp", "fsdp"), axis=0, tiled=True),
-        lax.all_gather(w_key, ("dp", "fsdp"), axis=0, tiled=True),
-        lax.all_gather(w_value, ("dp", "fsdp"), axis=0, tiled=True),
-        lax.all_gather(w_gate, ("dp", "fsdp"), axis=0, tiled=True),
-        lax.all_gather(w_out, ("dp", "fsdp"), axis=0, tiled=True),
-    )
     d_branch = d_mid.astype(jnp.bfloat16)
     grad_out = weight_grad(gated, d_branch)
-    d_gated = matmul_tr(d_branch, wob)
+    d_gated = matmul_tr(d_branch, wo)
     d_pre_u = (d_gated * attn_normed * sig * (1.0 - sig)).astype(jnp.bfloat16)
     d_attn = scale_back(attn, scale_two, d_gated * sig).astype(jnp.bfloat16)
     d_blocks = to_blocks(d_attn)
@@ -150,21 +140,32 @@
     grad_value = weight_grad(normed, d_value)
     grad_gate = weight_grad(normed, d_pre_u)
     d_normed = (
-        matmul_tr(d_query, wqb)
-        + matmul_tr(d_key, wkb)
-        + matmul_tr(d_value, wvb)
-        + matmul_tr(d_pre_u, wub)
+        matmul_tr(d_query, wq)
+        + matmul_tr(d_key, wk)
+        + matmul_tr(d_value, wv)
+        + matmul_tr(d_pre_u, wu)
     )
     grad_tokens = (d_mid + scale_back(x, scale_one, d_normed)).astype(jnp.bfloat16)
-    shares = (
-        lax.psum_scatter(grad_query, ("dp", "fsdp"), scatter_dimension=0, tiled=True),
-        lax.psum_scatter(grad_key, ("dp", "fsdp"), scatter_dimension=0, tiled=True),
-        lax.psum_scatter(grad_value, ("dp", "fsdp"), scatter_dimension=0, tiled=True),
-        lax.psum_scatter(grad_gate, ("dp", "fsdp"), scatter_dimension=0, tiled=True),
-        lax.psum_scatter(grad_out, ("dp", "fsdp"), scatter_dimension=0, tiled=True),
-        lax.psum_scatter(grad_one, ("dp", "fsdp"), scatter_dimension=0, tiled=True),
-        lax.psum_scatter(grad_two, ("dp", "fsdp"), scatter_dimension=0, tiled=True),
-        lax.psum_scatter(grad_three, ("dp", "fsdp"), scatter_dimension=0, tiled=True),
+    half = jnp.bfloat16
+    ffn_grads = jnp.concatenate(
+        (
+            grad_one.astype(half),
+            grad_two.astype(half),
+            grad_three.astype(half).reshape(width, hidden),
+        ),
+        axis=1,
+    )
+    attn_grads = jnp.concatenate(
+        [g.astype(half) for g in (grad_query, grad_key, grad_value, grad_gate, grad_out)], axis=1
+    )
+    ffn_sum = lax.psum_scatter(ffn_grads, axes, scatter_dimension=0, tiled=True)
+    attn_sum = lax.psum_scatter(attn_grads, axes, scatter_dimension=0, tiled=True)
+    ffn_sum = ffn_sum.astype(jnp.float32)
+    attn_sum = attn_sum.astype(jnp.float32)
+    shares = tuple(attn_sum[:, i * width : (i + 1) * width] for i in range(5)) + (
+        ffn_sum[:, :hidden],
+        ffn_sum[:, hidden : 2 * hidden],
+        ffn_sum[:, 2 * hidden :].reshape(w_three.shape),
     )
     return (
         output,

time: 1800 us -> 793 us (0.44)
  waiting for transfers between devices: 1410 us -> 349 us
  local copies, waits for them, and re-layouts: 123 us -> 181 us
    reduce_scatter x8 -> x1, waiting for transfers between devices: 1050 us -> 191 us  [local(): ffn_sum = lax.psum_scatter(ffn_grads, axes, scatter_dimension=0, tiled=True)]
    all_gather x8 -> x2, waiting for transfers between devices: 360 us -> 93.4 us  [the longest x1 77.9 us: local(): lax.all_gather(jnp.concatenate((w_query, w_key, w_value, w_gate, w_out),...]
    unnamed x16 -> x5, waiting for transfers between devices: 5.16 us -> 64.1 us
    reshape x2 -> x6, local copies, waits for them, and re-layouts: 11.3 us -> 37.1 us  [the longest x1 11.8 us: local(): w3 = ffn_all[:, 2 * hidden:].reshape(hidden, width)]
    unnamed x72 -> x91, local copies, waits for them, and re-layouts: 27.8 us -> 49.3 us
  transfers between devices with their start and end apart: 16 -> 4, of which waited for: 16 -> 4; matrix products, arithmetic and copies ran while one was open for 14% -> 26% of each run, Pallas kernels for 0% -> 0%
where the time goes in v1:
time: 793 us; the launch traced here: 783 us
  waiting for transfers between devices  349 us (44%)
  matrix products  211 us (27%)
  local copies, waits for them, and re-layouts  181 us (23%)
  other arithmetic  27.5 us (3%)
  between operations  14.6 us (2%)
    reduce_scatter x1, waiting for transfers between devices, local(): ffn_sum = lax.psum_scatter(ffn_grads, axes, scatter_dimension=0, tiled=True)  191 us
    all_gather x1, waiting for transfers between devices, local(): lax.all_gather(jnp.concatenate((w_query, w_key, w_value, w_gate, w_out),...  77.9 us
    dot_general x8, matrix products, matmul(): return jnp.dot(left, right, preferred_element_type=jnp.float32)  76.7 us
    unnamed x5, waiting for transfers between devices  64.1 us
    dot_general x8, matrix products, matmul_tr(): lax.dot_general(left, right, (((1,), (1,)), ((), ())), preferred_element_...  52 us
    unnamed x91, local copies, waits for them, and re-layouts  49.3 us
    dot_general x8, matrix products, weight_grad(): lax.dot_general(left, right, (((0,), (0,)), ((), ())), preferred_element_...  48.5 us
    another operation x6, local copies, waits for them, and re-layouts  36.9 us
  transfers between devices with their start and end apart: 4, of which 4 were waited for; matrix products, arithmetic and copies ran while one was open for 26% of the time, Pallas kernels for 0%

profile of v1, /device:TPU:0, one launch (start us, length us, event | category | flops | bytes accessed | tf_op | source)
XLA Modules:
  0.0 782.6 jit_solution(7878872950076876467)
XLA Ops:
  23.3 77.9 %all-gather.3.cloned.1.call-done = bf16[1024,5120]{1,0:T(8,128)(2,1)} async-done(((bf16[32,5120]{1,0:T(8,128)(2,1)}), bf16[1024,5120]{1,0:T(8,128)(2,1)}) %all-gather.3.cloned.1.call-update) | async-done | bytes 10485776 | tf_op jit(solution)/shard_map/all_gather | solution.py:58
  118.8 7.2 multiply_convert_fusion.8
  137.6 7.9 %multiply_convert_fusion.7 = (bf16[1024,1024]{1,0:T(8,128)(2,1)}, f32[1024,1024]{1,0:T(8,128)}) fusion(bf16[1024,5120]{1,0:T(8,128)(2,1)} %all-gather.3.cloned.1.call-done, bf16[1024,1024]{0,1:T(8,128)(2,1)} %copy-done.7, f32[1024]{0:T(1024)S(1)} %add_rsqrt_fusion.1), kind=kOutput, calls=%fused_computation.51 | convolution fusion | flops 2155872256 | bytes 10489856 | tf_op jit(solution)/shard_map/dot_general | solution.py:35
  171.3 7.2 copy.159
  178.5 7.8 %reshape.207 = f32[1024,1024]{1,0:T(8,128)} reshape(f32[1,8,128,16,64]{4,3,2,1,0:T(8,128)} %copy.159) | data formatting | bytes 8388608 | tf_op jit(solution)/shard_map/reshape | solution.py:92
  186.3 8.6 %multiply_convert_fusion.6 = (bf16[1024,1024]{1,0:T(8,128)(2,1)S(1)}, f32[1024,1024]{1,0:T(8,128)}) fusion(f32[1024,1024]{1,0:T(8,128)} %reshape.207, f32[1024]{0:T(1024)S(1)} %rsqrt_bitcast_fusion, bf16[1024,5120]{1,0:T(8,128)(2,1)} %all-gather.3.cloned.1.call-done, bf16[1024,1024]{0,1:T(8,128)(2,1)} %copy-done.7, f32[1024]{0:T(1024)S(1)} %add_rsqrt_fusion.1), kind=kOutput, calls=%fused_computation.46 | convolution fusion | flops 2156920832 | bytes 14688256 | tf_op jit(solution)/shard_map/dot_general | solution.py:35
  204.0 15.5 %all-gather.5.cloned.1.call-done = bf16[1024,8448]{1,0:T(8,128)(2,1)} async-done(((bf16[32,8448]{1,0:T(8,128)(2,1)}), bf16[1024,8448]{1,0:T(8,128)(2,1)}) %all-gather.5.cloned.1.call-update) | async-done | bytes 17301520 | tf_op jit(solution)/shard_map/all_gather | solution.py:61
  225.0 11.8 %reshape.194 = bf16[2816,1024]{1,0:T(8,128)(2,1)} reshape(bf16[1024,2816]{1,0:T(8,128)(2,1)} %slice.71) | data formatting | bytes 11534336 | tf_op jit(solution)/shard_map/reshape | solution.py:70
  236.7 11.9 %fusion.61 = f32[2816,1024]{0,1:T(8,128)} fusion(bf16[2816,1024]{1,0:T(8,128)(2,1)} %reshape.194, bf16[1024,1024]{1,0:T(8,128)(2,1)} %param.19), kind=kOutput, calls=%fused_computation.105 | convolution fusion | flops 5905580032 | bytes 19398656 | tf_op jit(solution)/shard_map/dot_general | solution.py:39
  248.7 12.0 %fusion.8 = f32[1024,2816]{1,0:T(8,128)} fusion(bf16[1024,1024]{0,1:T(8,128)(2,1)S(1)} %copy-done.23, bf16[1024,8448]{1,0:T(8,128)(2,1)} %all-gather.5.cloned.1.call-done), kind=kOutput, calls=%fused_computation.21 | convolution fusion | flops 5905580032 | bytes 19398656 | tf_op jit(solution)/shard_map/dot_general | solution.py:35
  260.7 18.7 %fusion = (bf16[1024,2816]{1,0:T(8,128)(2,1)}, bf16[1024,2816]{1,0:T(8,128)(2,1)}, bf16[1024,2816]{1,0:T(8,128)(2,1)}) fusion(f32[2816,1024]{0,1:T(8,128)} %fusion.61, f32[1024,2816]{1,0:T(8,128)} %fusion.8, bf16[1024,1024]{0,1:T(8,128)(2,1)} %multiply_convert_fusion.9, bf16[1024,8448]{1,0:T(8,128)(2,1)} %all-gather.5.cloned.1.call-done), kind=kOutput, calls=%fused_computation.3 | convolution fusion | flops 5922881536 | bytes 48234496 | tf_op jit(solution)/shard_map/dot_general | solution.py:35
  279.4 10.0 %fusion.2 = f32[1024,1024]{0,1:T(8,128)S(1)} fusion(bf16[1024,2816]{1,0:T(8,128)(2,1)} %get-tuple-element.43, bf16[1024,8448]{1,0:T(8,128)(2,1)} %all-gather.5.cloned.1.call-done), kind=kOutput, calls=%fused_computation.15 | convolution fusion | flops 5905580032 | bytes 15728640 | tf_op jit(solution)/shard_map/dot_general | solution.py:39
  289.5 8.5 %multiply_reduce_fusion.1 = (f32[1024]{0:T(1024)S(1)}, f32[1024,1024]{0,1:T(8,128)S(1)}) fusion(f32[1024,1024]{0,1:T(8,128)S(1)} %copy-done.18, f32[1024,1024]{0,1:T(8,128)S(1)} %fusion.2, bf16[1024,2816]{1,0:T(8,128)(2,1)S(1)} %copy-done.25, bf16[1024,8448]{1,0:T(8,128)(2,1)} %all-gather.5.cloned.1.call-done), kind=kOutput, calls=%fused_computation.43 | convolution fusion | flops 5908724736 | bytes 24121344 | tf_op jit(solution)/shard_map/dot_general | solution.py:39
  345.2 7.2 copy.149
  352.4 7.8 reshape.200
  372.8 8.0 %reshape.201 = f32[1024,1024]{1,0:T(8,128)} reshape(f32[1,8,128,16,64]{4,3,2,1,0:T(8,128)} %copy.150) | data formatting | bytes 8388608 | tf_op jit(solution)/shard_map/reshape | solution.py:136
  407.5 13.9 %copy.151 = bf16[1024,5120]{1,0:T(8,128)(2,1)} copy(bf16[1024,5120]{0,1:T(8,128)(2,1)} %convert_dynamic-update-slice_fusion) | data formatting | bytes 20971520
  421.5 11.0 %convolution_convert_fusion = bf16[2816,1024]{1,0:T(8,128)(2,1)} fusion(bf16[1024,2816]{1,0:T(8,128)(2,1)} %get-tuple-element.44, bf16[1024,1024]{1,0:T(8,128)(2,1)} %param.19), kind=kOutput, calls=%fused_computation.12 | convolution fusion | flops 5908463616 | bytes 13631488 | tf_op jit(solution)/shard_map/dot_general | solution.py:45
  432.5 11.7 %reshape.198 = bf16[1024,2816]{1,0:T(8,128)(2,1)} reshape(bf16[2816,1024]{1,0:T(8,128)(2,1)} %convolution_convert_fusion) | data formatting | bytes 11534336 | tf_op jit(solution)/shard_map/reshape | solution.py:154
  444.2 9.5 %convolution_convert_fusion.1 = bf16[1024,2816]{1,0:T(8,128)(2,1)S(1)} fusion(bf16[1024,1024]{0,1:T(8,128)(2,1)} %multiply_convert_fusion.9, bf16[1024,2816]{1,0:T(8,128)(2,1)} %get-tuple-element.43), kind=kOutput, calls=%fused_computation.13 | convolution fusion | flops 5908463616 | bytes 13631488 | tf_op jit(solution)/shard_map/dot_general | solution.py:45
  453.7 9.2 %convolution_convert_fusion.2 = bf16[1024,2816]{1,0:T(8,128)(2,1)S(1)} fusion(bf16[1024,1024]{0,1:T(8,128)(2,1)S(1)} %copy-done.24, bf16[1024,2816]{1,0:T(8,128)(2,1)} %get-tuple-element.42), kind=kOutput, calls=%fused_computation.14 | convolution fusion | flops 5908463616 | bytes 13631488 | tf_op jit(solution)/shard_map/dot_general | solution.py:45
  469.8 11.9 %add_convert_fusion.1 = bf16[1024,1024]{0,1:T(8,128)(2,1)} fusion(f32[1024,1024]{0,1:T(8,128)} %copy-done.17, bf16[1024,2816]{1,0:T(8,128)(2,1)} %get-tuple-element.44, bf16[2816,1024]{1,0:T(8,128)(2,1)} %reshape.194), kind=kOutput, calls=%fused_computation.44 | convolution fusion | flops 5907677184 | bytes 17825792 | tf_op jit(solution)/shard_map/dot_general | solution.py:35
  509.8 64.0 %reduce-scatter.7.cloned.1.call-done = bf16[32,5120]{1,0:T(8,128)(2,1)} async-done(((bf16[1024,5120]{1,0:T(8,128)(2,1)}), bf16[32,5120]{1,0:T(8,128)(2,1)}) %reduce-scatter.7.cloned.1.call-update) | async-done | bytes 327696
  581.6 191.4 %reduce-scatter.5.cloned.1.call-done = bf16[32,8448]{1,0:T(8,128)(2,1)} async-done(((bf16[1024,8448]{1,0:T(8,128)(2,1)}), bf16[32,8448]{1,0:T(8,128)(2,1)}) %reduce-scatter.5.cloned.1.call-update) | async-done | bytes 540688 | tf_op jit(solution)/shard_map/reduce_scatter | solution.py:161
  (157 shorter events, 217.4 us)
Async XLA Ops:
  7.2 94.0 %all-gather.3.cloned.1.call-start = ((), (), s32[]{:S(2)}) async-start(), calls=%async_computation.2 | async-start | bytes 10813440 | tf_op jit(solution)/shard_map/all_gather | solution.py:58
  12.2 207.3 %all-gather.5.cloned.1.call-start = ((), (), s32[]{:S(2)}) async-start(), calls=%async_computation.3 | async-start | bytes 17842176 | tf_op jit(solution)/shard_map/all_gather | solution.py:61
  15.3 558.6 %reduce-scatter.7.cloned.1.call-start = ((), (), s32[]{:S(2)}) async-start(), calls=%async_computation.5 | async-start | bytes 10813440
  18.2 100.6 %copy-start.7 = (bf16[1024,1024]{0,1:T(8,128)(2,1)}, bf16[1024,1024]{0,1:T(8,128)(2,1)S(1)}, u32[]{:S(2)}) copy-start(bf16[1024,1024]{0,1:T(8,128)(2,1)S(1)} %copy.99) | copy-start | bytes 6291460
  162.7 5.3 copy-start.15
  186.3 8.6 %copy-start.8 = (bf16[1024,1024]{0,1:T(8,128)(2,1)S(1)}, bf16[1024,1024]{0,1:T(8,128)(2,1)}, u32[]{:S(2)}) copy-start(bf16[1024,1024]{0,1:T(8,128)(2,1)} %copy-done.7) | copy-start | bytes 6291460
  195.0 5.1 copy-start.34
  236.7 11.9 %copy-start.23 = (bf16[1024,1024]{0,1:T(8,128)(2,1)S(1)}, bf16[1024,1024]{0,1:T(8,128)(2,1)}, u32[]{:S(2)}) copy-start(bf16[1024,1024]{0,1:T(8,128)(2,1)} %multiply_convert_fusion.9) | copy-start | bytes 6291460
  279.4 10.0 %copy-start.18 = (f32[1024,1024]{0,1:T(8,128)S(1)}, f32[1024,1024]{0,1:T(8,128)}, u32[]{:S(2)}) copy-start(f32[1024,1024]{0,1:T(8,128)} %copy-done.17) | copy-start | bytes 12582916
  279.4 10.1 %copy-start.25 = (bf16[1024,2816]{1,0:T(8,128)(2,1)S(1)}, bf16[1024,2816]{1,0:T(8,128)(2,1)}, u32[]{:S(2)}) copy-start(bf16[1024,2816]{1,0:T(8,128)(2,1)} %get-tuple-element.42) | copy-start | bytes 17301508
  289.5 8.6 %copy-start.26 = (bf16[1024,1024]{0,1:T(8,128)(2,1)S(1)}, bf16[1024,1024]{0,1:T(8,128)(2,1)}, u32[]{:S(2)}) copy-start(bf16[1024,1024]{0,1:T(8,128)(2,1)} %copy.114) | copy-start | bytes 6291460
  298.1 5.0 copy-start.20
  299.7 7.4 copy-start.10
  322.8 4.2 copy-start
  352.3 7.8 copy-start.5
  380.8 5.1 copy-start.9
  385.9 5.0 copy-start.27
  421.4 351.6 %reduce-scatter.5.cloned.1.call-start = ((), (), s32[]{:S(2)}) async-start(), calls=%async_computation.4 | async-start | bytes 17842176 | tf_op jit(solution)/shard_map/reduce_scatter | solution.py:161
  444.2 9.5 %copy-start.24 = (bf16[1024,1024]{0,1:T(8,128)(2,1)S(1)}, bf16[1024,1024]{0,1:T(8,128)(2,1)}, u32[]{:S(2)}) copy-start(bf16[1024,1024]{0,1:T(8,128)(2,1)} %multiply_convert_fusion.9) | copy-start | bytes 6291460
  444.2 18.7 %slice-start = ((s8[5767168]{0:T(1024)(128)(4,1)}), s8[4194304]{0:T(1024)(128)(4,1)S(1)}, s32[]{:S(2)}) async-start(s8[5767168]{0:T(1024)(128)(4,1)} %bitcast.91), calls=%async_computation.6 | async-start | bytes 8388608
  453.7 9.2 %slice-start.1 = ((s8[5767168]{0:T(1024)(128)(4,1)}), s8[1572864]{0:T(1024)(128)(4,1)S(1)}, s32[]{:S(2)}) async-start(s8[5767168]{0:T(1024)(128)(4,1)} %bitcast.91), calls=%async_computation.7 | async-start | bytes 3145728
  485.6 4.7 copy-start.29
  490.3 4.2 copy-start.31
  498.7 4.5 copy-start.12
  (18 other events, 50.4 us)
Sparse Core Ops, SparseCore 0:
  12.3 88.8 all-gather.2
  104.1 115.3 all-gather.4
  421.5 152.2 reduce-scatter.6
  580.1 192.8 reduce-scatter.4

commit v2 on v1

--- a/solution.py
+++ b/solution.py
@@ -1,15 +1,21 @@
+import functools
+
 import jax
 import jax.numpy as jnp
 from jax import lax
+from jax.experimental import pallas as pl
+from jax.experimental.pallas import tpu as pltpu
 from jax.sharding import PartitionSpec as P
 
 HEADS = 16
 HEAD = 64
 BLOCK = 128
 SEQ = 1024
-
-
+SPAN = 256
 EPS = 1e-06
+MESH = pl.DeviceIdType.MESH
+F32 = jnp.float32
+BF16 = jnp.bfloat16
 
 
 def row_scale(value):
@@ -47,11 +53,81 @@
     )
 
 
+class Cube:
+    def __init__(self, nd, nf):
+        self.nd, self.nf = nd, nf
+        self.kd, self.kf = nd.bit_length() - 1, nf.bit_length() - 1
+        self.k = self.kd + self.kf
+        top = [self.kf - 1, self.kf - 2]
+        outer = list(range(self.kf, self.k))
+        mid = list(range(self.kf - 3, 0, -1))
+        self.kinds = (
+            (top + outer + mid + [0], top + mid + outer + [0]),
+            (outer + top + mid + [0], mid + top + outer + [0]),
+        )
+
+    def place(self):
+        self.x, self.f = lax.axis_index("dp"), lax.axis_index("fsdp")
+        index = self.x * self.nf + self.f
+        self.bits = [(index // (1 << b)) % 2 for b in range(self.k)]
+
+    def partner(self, b):
+        step = 1 - 2 * self.bits[b]
+        if b < self.kf:
+            return (self.x, self.f + step * (1 << b))
+        return (self.x + step * (1 << (b - self.kf)), self.f)
+
+    def at(self, free, flip=None):
+        return tuple(
+            slice(None) if b in free else (1 - self.bits[b] if b == flip else self.bits[b])
+            for b in range(self.k - 1, -1, -1)
+        )
+
+    def barrier(self):
+        sem = pltpu.get_barrier_semaphore()
+        for b in range(self.k):
+            pl.semaphore_signal(sem, inc=1, device_id=self.partner(b), device_id_type=MESH)
+        pl.semaphore_wait(sem, self.k)
+
+
+def at_row(i, size):
+    return pl.ds(pl.multiple_of(i * size, size), size)
+
+
+def head_masks(shape):
+    lane = lax.broadcasted_iota(jnp.int32, shape, len(shape) - 1)
+    return lane < HEAD
+
+
+def two_heads(value):
+    low = head_masks(value.shape)
+    zero = jnp.zeros_like(value)
+    return jnp.concatenate([jnp.where(low, value, zero), jnp.where(low, zero, value)], axis=0)
+
+
+def pick_heads(value):
+    rows = value.shape[0] // 2
+    upper, lower = value[:rows], value[rows:]
+    return jnp.where(head_masks(upper.shape), upper, lower)
+
+
+def causal_pair():
+    row = lax.broadcasted_iota(jnp.int32, (SPAN, 2 * SPAN), 0)
+    col = lax.broadcasted_iota(jnp.int32, (SPAN, 2 * SPAN), 1)
+    return row >= jnp.where(col >= SPAN, col - SPAN, col)
+
+
+def same_head(value):
+    row = lax.broadcasted_iota(jnp.int32, value.shape, 0)
+    col = lax.broadcasted_iota(jnp.int32, value.shape, 1)
+    return jnp.where((row < HEAD) == (col < HEAD), value, jnp.zeros_like(value))
+
+
 def to_blocks(value):
     return value.reshape(-1, SEQ // BLOCK, BLOCK, HEADS, HEAD)
 
 
-def local(tokens, w_query, w_key, w_value, w_gate, w_out, w_one, w_two, w_three, cotangent):
+def plain_local(tokens, w_query, w_key, w_value, w_gate, w_out, w_one, w_two, w_three, cotangent):
     axes = ("dp", "fsdp")
     rows, width = w_query.shape
     hidden = w_one.shape[1]
@@ -181,29 +257,447 @@
     )
 
 
+class Copies:
+    def __init__(self, sems):
+        self.sems, self.count = sems, 0
+
+    def start(self, src, dst):
+        copy = pltpu.make_async_copy(src, dst, self.sems.at[self.count])
+        self.count += 1
+        copy.start()
+        return copy
+
+
+def forward_chunks(width, hidden):
+    chunks = []
+    for t in range(5):
+        chunks += [(t, c, width // 2) for c in range(0, width, width // 2)]
+    for c in range(0, hidden, width):
+        size = min(width, hidden - c)
+        chunks += [(5, c, size), (6, c, size)]
+    chunks += [(7, c, 256) for c in range(0, width, 256)]
+    return chunks
+
+
+SLOTS, SLOTS3, SPACING = 5, 3, 2
+ACTS = ("nrm", "q", "sq", "k", "sk", "v", "u", "att", "y", "mid", "n2", "g1", "g2", "prod", "out")
+
+
+def forward_kernel(cube, chunks, *refs):
+    tok, shards = refs[0], refs[1:9]
+    weights = refs[9:17]
+    acts = dict(zip(ACTS, refs[17 : 17 + len(ACTS)]))
+    (nb, a1, a2, a3, fu, fa, fm, stage, stage3, send, recv, own, local) = refs[17 + len(ACTS) :]
+    cube.place()
+    core, k, n = cube.bits[0], cube.k, len(chunks)
+    width = tok.shape[1]
+    mine = []
+    for t in range(8):
+        mine.append(pltpu.make_async_copy(shards[t], weights[t].at[cube.at(())], own.at[t]))
+        mine[-1].start()
+    cube.barrier()
+    copies = Copies(local)
+
+
+    def copy(c, s, v):
+        t, c0, w = chunks[c]
+        order = cube.kinds[c % 2][v]
+        where = cube.at(order[:s]) + (slice(None), pl.ds(c0, w))
+        src = shards[t].at[:, pl.ds(c0, w)] if s == 0 else weights[t].at[where]
+        return pltpu.make_async_remote_copy(
+            src_ref=src,
+            dst_ref=weights[t].at[where],
+            send_sem=send.at[c, s],
+            recv_sem=recv.at[c, s],
+            device_id=cube.partner(order[s]),
+            device_id_type=MESH,
+        )
+
+    def both(c, s, act):
+        first, second = cube.kinds[c % 2]
+        if first[s] == second[s] and set(first[:s]) == set(second[:s]):
+            act(copy(c, s, 0))
+        else:
+
+            @pl.when(core == 0)
+            def _():
+                act(copy(c, s, 0))
+
+            @pl.when(core == 1)
+            def _():
+                act(copy(c, s, 1))
+
+
+    whole = (slice(None),) * (k + 1)
+    pending = {}
+
+    def out_of(name, src):
+        pending[name] = copies.start(src, acts[name])
+
+    def settle(*names):
+        for name in names:
+            if name in pending:
+                pending.pop(name).wait()
+
+    def cols(ref, c, w):
+        return ref[whole + (pl.ds(pl.multiple_of(c, 256), w),)].reshape(-1, w)
+
+    def tiles(total, body):
+        def step(i, carry):
+            body(i // 2, i % 2)
+            return carry
+
+        lax.fori_loop(0, total // 256 * 2, step, 0)
+
+    def rows(body, size=128):
+        def step(i, carry):
+            body(at_row(i, size))
+            return carry
+
+        lax.fori_loop(0, SEQ // size, step, 0)
+
+    def norm_one():
+        def body(r):
+            x = tok[r, :].astype(F32)
+            nb[r, :] = (x * row_scale(x)).astype(BF16)
+
+        rows(body)
+        out_of("nrm", nb)
+
+    def project(t, c0, w, ref):
+        def body(j, h):
+            r = at_row(h, 512)
+            to = pl.ds(pl.multiple_of(c0 + j * 256, 256), 256)
+            acc = matmul(nb[r, :], cols(ref, j * 256, 256))
+            if t == 3:
+                fu[r, to] = acc
+            elif t == 2:
+                a3[r, to] = acc.astype(BF16)
+            else:
+                slope_to = pl.ds(pl.multiple_of(width + c0 + j * 256, 256), 256)
+                sig = logistic(acc)
+                dst = a1 if t == 0 else a2
+                dst[r, to] = (acc * sig).astype(BF16)
+                dst[r, slope_to] = (sig * (1.0 + acc * (1.0 - sig))).astype(BF16)
+
+        tiles(w, body)
+        if c0 + w == width:
+            if t == 3:
+                out_of("u", fu)
+            elif t == 2:
+                out_of("v", a3.at[:, pl.ds(0, width)])
+            else:
+                src = a1 if t == 0 else a2
+                out_of("qk"[t], src.at[:, pl.ds(0, width)])
+                out_of(("sq", "sk")[t], src.at[:, pl.ds(width, width)])
+
+    def attend(first, last):
+        mask = causal_pair()
+
+        def pair(p, carry):
+            at = pl.ds(pl.multiple_of(p * 128, 128), 128)
+            state = jnp.zeros((128, 128), F32)
+            for b in range(SEQ // SPAN):
+                r = pl.ds(b * SPAN, SPAN)
+                q, kk, v = a1[r, at], a2[r, at], a3[r, at]
+                scores = jnp.where(mask, matmul_tr(q, two_heads(kk)), 0.0).astype(BF16)
+                acc = matmul(scores, two_heads(v))
+                if b > 0:
+                    acc += matmul(q, state.astype(BF16))
+                fa[r, at] = acc
+                if b + 1 < SEQ // SPAN:
+                    state += same_head(weight_grad(kk, v))
+            return carry
+
+        lax.fori_loop(first, last, pair, 0)
+        if last == width // 128:
+            out_of("att", fa)
+
+    def gate():
+        def body(r):
+            attn = fa[r, :]
+            a3[r, pl.ds(width, width)] = (attn * row_scale(attn) * logistic(fu[r, :])).astype(BF16)
+
+        rows(body)
+        out_of("y", a3.at[:, pl.ds(width, width)])
+
+    def project_out(c0, w, ref):
+        def body(j, h):
+            r = at_row(h, 512)
+            to = pl.ds(pl.multiple_of(c0 + j * 256, 256), 256)
+            fm[r, to] = tok[r, to].astype(F32) + matmul(
+                a3[r, pl.ds(width, width)], cols(ref, j * 256, 256)
+            )
+
+        tiles(w, body)
+
+    def norm_two():
+        settle("nrm")
+
+        def body(r):
+            mid = fm[r, :]
+            nb[r, :] = (mid * row_scale(mid)).astype(BF16)
+
+        rows(body)
+        out_of("mid", fm)
+        out_of("n2", nb)
+        settle("q", "sq", "k", "sk", "v", "y")
+
+    def hidden(c0, w, one, two):
+        def body(j, h):
+            r = at_row(h, 512)
+            to = pl.ds(pl.multiple_of(c0 + j * 256, 256), 256)
+            first = matmul(nb[r, :], cols(one, j * 256, 256))
+            second = matmul(nb[r, :], cols(two, j * 256, 256))
+            a1[r, to] = first.astype(BF16)
+            a2[r, to] = second.astype(BF16)
+            a3[r, to] = (first * second).astype(BF16)
+
+        tiles(w, body)
+        if c0 + w == a1.shape[1]:
+            out_of("g1", a1)
+            out_of("g2", a2)
+            out_of("prod", a3)
+            settle("n2")
+
+    def down(c0, w, ref):
+        def body(j, h):
+            r = at_row(h, 512)
+            to = pl.ds(pl.multiple_of(c0 + j * 256, 256), 256)
+            nb[r, to] = (fm[r, to] + matmul(a3[r, :], cols(ref, j * 256, 256))).astype(BF16)
+
+        tiles(w, body)
+        if c0 + w == width:
+            out_of("out", nb)
+
+    index = {(t, c0): i for i, (t, c0, w) in enumerate(chunks)}
+    items = [((), norm_one)]
+    for i, (t, c0, w) in enumerate(chunks):
+        last = c0 + w == width
+        if t < 4:
+            items.append(((i,), functools.partial(project, t, c0, w)))
+            if t == 2 and last:
+                items += [((), functools.partial(attend, 0, 4)), ((), functools.partial(attend, 4, 8))]
+            if t == 3 and last:
+                items.append(((), gate))
+        elif t == 4:
+            items.append(((i,), functools.partial(project_out, c0, w)))
+            if last:
+                items.append(((), norm_two))
+        elif t == 5:
+            items.append(((i, index[6, c0]), functools.partial(hidden, c0, w)))
+        elif t == 7:
+            items.append(((i,), functools.partial(down, c0, w)))
+
+    free = {False: list(range(SLOTS)), True: list(range(SLOTS3))}
+    arrived, staged = [], {}
+
+    def stage_some(tick):
+        while arrived and free[chunks[arrived[0]][0] == 7]:
+            c = arrived.pop(0)
+            t, c0, w = chunks[c]
+            slot = free[t == 7].pop(0)
+            dst = (stage3 if t == 7 else stage).at[(slot,) + whole + (pl.ds(0, w),)]
+            cp = copies.start(weights[t].at[whole + (pl.ds(c0, w),)], dst)
+            staged[c] = (tick, slot, cp)
+
+    def run(tick, budget):
+        while items and budget > 0:
+            needs, act = items[0]
+            if any(c not in staged or staged[c][0] >= tick for c in needs):
+                return
+            items.pop(0)
+            given = []
+            for c in needs:
+                _, slot, cp = staged[c]
+                cp.wait()
+                given.append((stage3 if chunks[c][0] == 7 else stage).at[slot])
+            act(*given)
+            for c in needs:
+                free[chunks[c][0] == 7].append(staged[c][1])
+            budget -= 1
+
+    settled = set()
+    ticks = n + k * SPACING
+    for tick in range(ticks):
+        for c in range(n):
+            d = tick - c
+            if d < 0 or d % SPACING or d // SPACING > k:
+                continue
+            s = d // SPACING
+            if s > 0:
+                both(c, s - 1, lambda cp: cp.wait_recv())
+            if s == 1 and chunks[c][0] not in settled:
+                settled.add(chunks[c][0])
+                mine[chunks[c][0]].wait()
+            if s < k:
+                both(c, s, lambda cp: cp.start())
+            else:
+                arrived.append(c)
+        run(tick, 2)
+        stage_some(tick)
+    tick = ticks
+    while items:
+        run(tick, 1)
+        stage_some(tick)
+        tick += 1
+    for c in range(n):
+        for s in range(k):
+            both(c, s, lambda cp: cp.wait_send())
+    settle(*list(pending))
+
+
+def forward(cube, tokens, shards):
+    width, hidden = tokens.shape[1], shards[5].shape[1]
+    chunks = forward_chunks(width, hidden)
+    n, k = len(chunks), cube.k
+    cubed = (2,) * k
+    act = lambda dtype: jax.ShapeDtypeStruct(tokens.shape, dtype)
+    kinds = dict.fromkeys(("u", "att", "mid"), act(F32))
+    kinds.update(dict.fromkeys(("g1", "g2", "prod"), jax.ShapeDtypeStruct((SEQ, hidden), BF16)))
+    outs = [jax.ShapeDtypeStruct(cubed + s.shape, s.dtype) for s in shards]
+    outs += [kinds.get(name, act(BF16)) for name in ACTS]
+    got = pl.pallas_call(
+        functools.partial(forward_kernel, cube, chunks),
+        out_shape=tuple(outs),
+        in_specs=[pl.BlockSpec(memory_space=pltpu.VMEM)] * 9,
+        out_specs=tuple([pl.BlockSpec(memory_space=pl.ANY)] * len(outs)),
+        scratch_shapes=[
+            pltpu.VMEM(tokens.shape, BF16),
+            pltpu.VMEM((SEQ, hidden), BF16),
+            pltpu.VMEM((SEQ, hidden), BF16),
+            pltpu.VMEM((SEQ, hidden), BF16),
+            pltpu.VMEM(tokens.shape, F32),
+            pltpu.VMEM(tokens.shape, F32),
+            pltpu.VMEM(tokens.shape, F32),
+            pltpu.VMEM((SLOTS,) + cubed + (shards[0].shape[0], width), BF16),
+            pltpu.VMEM((SLOTS3,) + cubed + (shards[7].shape[0], 256), BF16),
+            pltpu.SemaphoreType.DMA((n, k)),
+            pltpu.SemaphoreType.DMA((n, k)),
+            pltpu.SemaphoreType.DMA((8,)),
+            pltpu.SemaphoreType.DMA((n + len(ACTS),)),
+        ],
+        compiler_params=pltpu.CompilerParams(
+            collective_id=0, has_side_effects=True, vmem_limit_bytes=64 * 1024 * 1024 - 65536
+        ),
+        name="gather_and_forward",
+    )(tokens, *shards)
+    return got[:8], dict(zip(ACTS, got[8:]))
+
+
+def local(cube, tokens, w_query, w_key, w_value, w_gate, w_out, w_one, w_two, w_three, cotangent):
+    shards = (w_query, w_key, w_value, w_gate, w_out, w_one, w_two, w_three)
+    axes = ("dp", "fsdp")
+    width, hidden = w_one.shape[0] * cube.nd * cube.nf, w_one.shape[1]
+    gathered, acts = forward(cube, tokens, shards)
+    wq, wk, wv, wu, wo, w1, w2, w3 = (w.reshape(-1, w.shape[-1]) for w in gathered)
+    x = tokens.astype(F32)
+    scale_one = row_scale(x)
+    normed, normed_two, gated, product = acts["nrm"], acts["n2"], acts["y"], acts["prod"]
+    first, second = acts["g1"].astype(F32), acts["g2"].astype(F32)
+    mid, attn, output = acts["mid"], acts["att"], acts["out"]
+    scale_two, scale_three = row_scale(attn), row_scale(mid)
+    attn_normed, sig = attn * scale_two, logistic(acts["u"])
+    q_blocks, k_blocks, v_blocks = to_blocks(acts["q"]), to_blocks(acts["k"]), to_blocks(acts["v"])
+    causal = jnp.tril(jnp.ones((BLOCK, BLOCK), jnp.float32))
+    scores = (
+        jnp.einsum("bnchd,bnehd->bnhce", q_blocks, k_blocks, preferred_element_type=jnp.float32)
+        * causal
+    ).astype(jnp.bfloat16)
+    block_kv = jnp.einsum(
+        "bnchd,bnche->bnhde", k_blocks, v_blocks, preferred_element_type=jnp.float32
+    )
+    state = (jnp.cumsum(block_kv, axis=1) - block_kv).astype(jnp.bfloat16)
+    grad_three = weight_grad(product, cotangent)
+    dprod = matmul_tr(cotangent, w3)
+    d_first = (dprod * second).astype(jnp.bfloat16)
+    d_second = (dprod * first).astype(jnp.bfloat16)
+    grad_one = weight_grad(normed_two, d_first)
+    grad_two = weight_grad(normed_two, d_second)
+    d_normed_two = matmul_tr(d_first, w1) + matmul_tr(d_second, w2)
+    d_mid = cotangent.astype(jnp.float32) + scale_back(mid, scale_three, d_normed_two)
+    d_branch = d_mid.astype(jnp.bfloat16)
+    grad_out = weight_grad(gated, d_branch)
+    d_gated = matmul_tr(d_branch, wo)
+    d_pre_u = (d_gated * attn_normed * sig * (1.0 - sig)).astype(jnp.bfloat16)
+    d_attn = scale_back(attn, scale_two, d_gated * sig).astype(jnp.bfloat16)
+    d_blocks = to_blocks(d_attn)
+    d_scores = (
+        jnp.einsum("bnchd,bnehd->bnhce", d_blocks, v_blocks, preferred_element_type=jnp.float32)
+        * causal
+    ).astype(jnp.bfloat16)
+    d_state = jnp.einsum(
+        "bnchd,bnche->bnhde", q_blocks, d_blocks, preferred_element_type=jnp.float32
+    )
+    d_kv = (lax.cumsum(d_state, axis=1, reverse=True) - d_state).astype(jnp.bfloat16)
+    dq_full = jnp.einsum(
+        "bnhce,bnehd->bnchd", d_scores, k_blocks, preferred_element_type=jnp.float32
+    ) + jnp.einsum("bnche,bnhde->bnchd", d_blocks, state, preferred_element_type=jnp.float32)
+    dk_full = jnp.einsum(
+        "bnhce,bnchd->bnehd", d_scores, q_blocks, preferred_element_type=jnp.float32
+    ) + jnp.einsum("bnche,bnhde->bnchd", v_blocks, d_kv, preferred_element_type=jnp.float32)
+    dv_full = jnp.einsum(
+        "bnhce,bnchd->bnehd", scores, d_blocks, preferred_element_type=jnp.float32
+    ) + jnp.einsum("bnchd,bnhde->bnche", k_blocks, d_kv, preferred_element_type=jnp.float32)
+    d_query = (dq_full.reshape(tokens.shape) * acts["sq"]).astype(jnp.bfloat16)
+    d_key = (dk_full.reshape(tokens.shape) * acts["sk"]).astype(jnp.bfloat16)
+    d_value = dv_full.reshape(tokens.shape).astype(jnp.bfloat16)
+    grad_query = weight_grad(normed, d_query)
+    grad_key = weight_grad(normed, d_key)
+    grad_value = weight_grad(normed, d_value)
+    grad_gate = weight_grad(normed, d_pre_u)
+    d_normed = (
+        matmul_tr(d_query, wq)
+        + matmul_tr(d_key, wk)
+        + matmul_tr(d_value, wv)
+        + matmul_tr(d_pre_u, wu)
+    )
+    grad_tokens = (d_mid + scale_back(x, scale_one, d_normed)).astype(jnp.bfloat16)
+    half = jnp.bfloat16
+    ffn_grads = jnp.concatenate(
+        (
+            grad_one.astype(half),
+            grad_two.astype(half),
+            grad_three.astype(half).reshape(width, hidden),
+        ),
+        axis=1,
+    )
+    attn_grads = jnp.concatenate(
+        [g.astype(half) for g in (grad_query, grad_key, grad_value, grad_gate, grad_out)], axis=1
+    )
+    ffn_sum = lax.psum_scatter(ffn_grads, axes, scatter_dimension=0, tiled=True)
+    attn_sum = lax.psum_scatter(attn_grads, axes, scatter_dimension=0, tiled=True)
+    ffn_sum = ffn_sum.astype(jnp.float32)
+    attn_sum = attn_sum.astype(jnp.float32)
+    shares = tuple(attn_sum[:, i * width : (i + 1) * width] for i in range(5)) + (
+        ffn_sum[:, :hidden],
+        ffn_sum[:, hidden : 2 * hidden],
+        ffn_sum[:, 2 * hidden :].reshape(w_three.shape),
+    )
+    return (
+        output,
+        grad_tokens,
+        shares[0],
+        shares[1],
+        shares[2],
+        shares[3],
+        shares[4],
+        shares[5],
+        shares[6],
+        shares[7],
+    )
+
+
 def solution(mesh):
-    in_specs = (
-        P(("dp", "fsdp"), None),
-        P(("dp", "fsdp"), None),
-        P(("dp", "fsdp"), None),
-        P(("dp", "fsdp"), None),
-        P(("dp", "fsdp"), None),
-        P(("dp", "fsdp"), None),
-        P(("dp", "fsdp"), None),
-        P(("dp", "fsdp"), None),
-        P(("dp", "fsdp"), None),
-        P(("dp", "fsdp"), None),
-    )
-    out_specs = (
-        P(("dp", "fsdp"), None),
-        P(("dp", "fsdp"), None),
-        P(("dp", "fsdp"), None),
-        P(("dp", "fsdp"), None),
-        P(("dp", "fsdp"), None),
-        P(("dp", "fsdp"), None),
-        P(("dp", "fsdp"), None),
-        P(("dp", "fsdp"), None),
-        P(("dp", "fsdp"), None),
-        P(("dp", "fsdp"), None),
-    )
-    return jax.shard_map(local, mesh=mesh, in_specs=in_specs, out_specs=out_specs, check_vma=False)
+    nd, nf = mesh.shape["dp"], mesh.shape["fsdp"]
+    rows = P(("dp", "fsdp"), None)
+
+    def step(*args):
+        fits = args[1].shape[0] % 16 == 0 and args[8].shape[0] % 8 == 0 and args[0].shape[0] == SEQ
+        if fits:
+            return local(Cube(nd, nf), *args)
+        return plain_local(*args)
+
+    return jax.shard_map(
+        step, mesh=mesh, in_specs=(rows,) * 10, out_specs=(rows,) * 10, check_vma=False
+    )

time: 793 us -> 721 us (0.909)
  Pallas kernels: 0 us -> 136 us
  waiting for transfers between devices: 349 us -> 263 us
  matrix products: 211 us -> 144 us
  local copies, waits for them, and re-layouts: 181 us -> 121 us
    pallas_call x0 -> x1, Pallas kernels: none -> 136 us  [forward(): pl.pallas_call(functools.partial(forward_kernel, cube, chunks), out_shape...]
    all_gather x2 -> x0, waiting for transfers between devices: 93.4 us -> none  [the longest x1 77.9 us: local(): lax.all_gather(jnp.concatenate((w_query, w_key, w_value, w_gate, w_out),...]
    dot_general x11 -> x0, matrix products: 84.4 us -> none  [the longest x8 76.7 us: matmul(): return jnp.dot(left, right, preferred_element_type=jnp.float32)]
    reshape x10 -> x6, local copies, waits for them, and re-layouts: 69.7 us -> 39.7 us  [the longest x2 14.9 us: local(): d_key = (dk_full.reshape(tokens.shape) * acts['sk']).astype(jnp.bfloat16)]
    unnamed x91 -> x94, local copies, waits for them, and re-layouts: 49.3 us -> 31.1 us
    dot_general x8, matrix products: 48.5 us -> 58.3 us  [weight_grad(): lax.dot_general(left, right, (((0,), (0,)), ((), ())), preferred_element_...]
    convert_element_type x3 -> x0, other arithmetic: 8.56 us -> none  [the longest x1 5.05 us: local(): (dq_full.reshape(x.shape) * swish_slope(pre_q)).astype(jnp.bfloat16)]
    unnamed x5 -> x3, waiting for transfers between devices: 64.1 us -> 72.2 us
  transfers between devices with their start and end apart: 4 -> 2, of which waited for: 4 -> 2; matrix products, arithmetic and copies ran while one was open for 26% -> 12% of each run, Pallas kernels for 0% -> 0%
where the time goes in v2:
time: 721 us; the launch traced here: 710 us
  waiting for transfers between devices  263 us (36%)
  matrix products  144 us (20%)
  Pallas kernels  136 us (19%)
  local copies, waits for them, and re-layouts  121 us (17%)
  other arithmetic  30.8 us (4%)
  between operations  14.7 us (2%)
    reduce_scatter x1, waiting for transfers between devices, local(): ffn_sum = lax.psum_scatter(ffn_grads, axes, scatter_dimension=0, tiled=True)  191 us
    pallas_call x1, Pallas kernels, forward(): pl.pallas_call(functools.partial(forward_kernel, cube, chunks), out_shape...  136 us
    unnamed x3, waiting for transfers between devices  72.2 us
    dot_general x8, matrix products, weight_grad(): lax.dot_general(left, right, (((0,), (0,)), ((), ())), preferred_element_...  58.3 us
    dot_general x8, matrix products, matmul_tr(): lax.dot_general(left, right, (((1,), (1,)), ((), ())), preferred_element_...  53 us
    another operation x6, local copies, waits for them, and re-layouts  31.5 us
    unnamed x94, local copies, waits for them, and re-layouts  31.1 us
    reshape x2, local copies, waits for them, and re-layouts, local(): d_key = (dk_full.reshape(tokens.shape) * acts['sk']).astype(jnp.bfloat16)  14.9 us
  transfers between devices with their start and end apart: 2, of which 2 were waited for; matrix products, arithmetic and copies ran while one was open for 12% of the time, Pallas kernels for 0%

profile of v2, /device:TPU:0, one launch (start us, length us, event | category | flops | bytes accessed | tf_op | source)
XLA Modules:
  0.0 710.0 jit_solution(1430659539719332589)
XLA Ops:
  7.9 136.3 %gather_and_forward.1 = (bf16[2,2,2,2,2,32,1024]{6,5,4,3,2,1,0:T(8,128)(2,1)}, bf16[2,2,2,2,2,32,1024]{6,5,4,3,2,1,0:T(8,128)(2,1)}, bf16[2,2,2,2,2,32,1024]{6,5...) custom-call(bf16[1024,1024]{1,0:T(8,128)(2,1)} %refs_0_.1, ...), custom_call_target="tpu_custom_call" | custom-call | tf_op jit(solution)/shard_map/gather_and_forward/pallas_call | solution.py:560
  144.1 9.6 %fusion.37 = f32[2816,1024]{0,1:T(8,128)S(1)} fusion(bf16[2816,1024]{1,0:T(8,128)(2,1)} %bitcast.96, bf16[1024,1024]{1,0:T(8,128)(2,1)} %param.19), kind=kOutput, calls=%fused_computation.70 | convolution fusion | flops 5905580032 | bytes 19398656 | tf_op jit(solution)/shard_map/dot_general | solution.py:45
  153.8 11.8 %fusion.32 = f32[1024,1024]{1,0:T(8,128)} fusion(bf16[1024,2816]{1,0:T(8,128)(2,1)} %bitcast.95, f32[2816,1024]{0,1:T(8,128)S(1)} %fusion.37, bf16[1024,2816]{1,0:T(8,128)(2,1)S(1)} %copy-done.9), kind=kOutput, calls=%fused_computation.66 | convolution fusion | flops 5914230784 | bytes 27262976 | tf_op jit(solution)/shard_map/dot_general | solution.py:45
  165.6 16.6 %multiply_reduce_fusion.3 = (f32[1024]{0:T(1024)S(1)}, f32[1024]{0:T(1024)S(1)}, f32[1024,1024]{1,0:T(8,128)}) fusion(f32[1024,1024]{1,0:T(8,128)} %get-tuple-element.34, f32[1024,1024]{1,0:T(8,128)} %fusion.32, bf16[1024,2816]{1,0:T(8,128)(2,1)} %bitcast.94, f32[2816,1024]{0,1:T(8,128)} %copy-done, bf16[1024,2816]{1,0:T(8,128)(2,1)} %get-tuple-element.38), kind=kOutput, calls=%fused_computation.38 | convolution fusion | flops 5919471616 | bytes 35659776 | tf_op jit(solution)/shard_map/dot_general | solution.py:45
  199.7 5.9 copy.92
  209.6 5.9 copy.101
  224.5 6.4 reshape.208
  230.9 6.2 copy.93
  237.1 5.4 fusion.41
  242.5 6.7 fusion.10
  275.6 7.1 copy.132
  282.7 7.8 %reshape.202 = f32[1024,1024]{1,0:T(8,128)} reshape(f32[1,8,128,16,64]{4,3,2,1,0:T(8,128)} %copy.132) | data formatting | bytes 8388608 | tf_op jit(solution)/shard_map/reshape | solution.py:642
  290.4 5.5 add_bitcast_fusion
  295.9 7.1 copy.133
  303.0 7.8 %reshape.203 = f32[1024,1024]{1,0:T(8,128)} reshape(f32[1,8,128,16,64]{4,3,2,1,0:T(8,128)} %copy.133) | data formatting | bytes 8388608 | tf_op jit(solution)/shard_map/reshape | solution.py:643
  310.8 6.8 convert_dynamic-update-slice_fusion.4
  332.7 13.7 %copy.134 = bf16[1024,5120]{1,0:T(8,128)(2,1)} copy(bf16[1024,5120]{0,1:T(8,128)(2,1)} %convert_dynamic-update-slice_fusion) | data formatting | bytes 20971520
  348.0 11.1 %convolution_convert_fusion = bf16[2816,1024]{1,0:T(8,128)(2,1)} fusion(bf16[1024,2816]{1,0:T(8,128)(2,1)} %get-tuple-element.55, bf16[1024,1024]{1,0:T(8,128)(2,1)S(1)} %copy-done.23), kind=kOutput, calls=%fused_computation.10 | convolution fusion | flops 5908463616 | bytes 13631488 | tf_op jit(solution)/shard_map/dot_general | solution.py:51
  359.1 11.9 %reshape.200 = bf16[1024,2816]{1,0:T(8,128)(2,1)} reshape(bf16[2816,1024]{1,0:T(8,128)(2,1)} %convolution_convert_fusion) | data formatting | bytes 11534336 | tf_op jit(solution)/shard_map/reshape | solution.py:661
  371.0 14.5 %convolution_convert_fusion.1 = bf16[1024,2816]{1,0:T(8,128)(2,1)} fusion(bf16[1024,1024]{1,0:T(8,128)(2,1)} %get-tuple-element.54, f32[2816,1024]{0,1:T(8,128)} %copy-done, bf16[1024,2816]{1,0:T(8,128)(2,1)} %get-tuple-element.38), kind=kOutput, calls=%fused_computation.11 | convolution fusion | flops 5917114368 | bytes 25165824 | tf_op jit(solution)/shard_map/dot_general | solution.py:51
  385.5 10.9 %convolution_convert_fusion.2 = bf16[1024,2816]{1,0:T(8,128)(2,1)} fusion(bf16[1024,1024]{1,0:T(8,128)(2,1)S(1)} %copy-done.6, f32[2816,1024]{0,1:T(8,128)S(1)} %bitcast.90, bf16[1024,2816]{1,0:T(8,128)(2,1)} %get-tuple-element.36), kind=kOutput, calls=%fused_computation.12 | convolution fusion | flops 5917114368 | bytes 25165824 | tf_op jit(solution)/shard_map/dot_general | solution.py:51
  396.4 14.0 %pad_maximum_fusion = bf16[1024,8448]{1,0:T(8,128)(2,1)} fusion(bf16[1024,2816]{1,0:T(8,128)(2,1)} %reshape.200, bf16[1024,2816]{1,0:T(8,128)(2,1)} %convolution_convert_fusion.1, bf16[1024,2816]{1,0:T(8,128)(2,1)} %convolution_convert_fusion.2), kind=kLoop, calls=%fused_computation | loop fusion | flops 51904512 | bytes 34603008 | tf_op jit(solution)/shard_map/concatenate | solution.py:657
  428.1 72.1 %reduce-scatter.7.cloned.1.call-done = bf16[32,5120]{1,0:T(8,128)(2,1)} async-done(((bf16[1024,5120]{1,0:T(8,128)(2,1)}), bf16[32,5120]{1,0:T(8,128)(2,1)}) %reduce-scatter.7.cloned.1.call-update) | async-done | bytes 327696
  508.0 190.8 %reduce-scatter.5.cloned.1.call-done = bf16[32,8448]{1,0:T(8,128)(2,1)} async-done(((bf16[1024,8448]{1,0:T(8,128)(2,1)}), bf16[32,8448]{1,0:T(8,128)(2,1)}) %reduce-scatter.5.cloned.1.call-update) | async-done | bytes 540688 | tf_op jit(solution)/shard_map/reduce_scatter | solution.py:668
  (132 shorter events, 103.5 us)
Async XLA Ops:
  7.2 493.1 %reduce-scatter.7.cloned.1.call-start = ((), (), s32[]{:S(2)}) async-start(), calls=%async_computation.3 | async-start | bytes 10813440
  144.1 9.6 %copy-start.9 = (bf16[1024,2816]{1,0:T(8,128)(2,1)S(1)}, bf16[1024,2816]{1,0:T(8,128)(2,1)}, u32[]{:S(2)}) copy-start(bf16[1024,2816]{1,0:T(8,128)(2,1)} %get-tuple-element.36) | copy-start | bytes 17301508
  153.7 11.9 %copy-start = (f32[2816,1024]{0,1:T(8,128)}, f32[2816,1024]{0,1:T(8,128)S(1)}, u32[]{:S(2)}) copy-start(f32[2816,1024]{0,1:T(8,128)S(1)} %fusion.37) | copy-start | bytes 34603012
  165.6 16.6 %copy-start.19 = (f32[1024,1024]{1,0:T(8,128)S(1)}, f32[1024,1024]{1,0:T(8,128)}, u32[]{:S(2)}) copy-start(f32[1024,1024]{1,0:T(8,128)} %get-tuple-element.34) | copy-start | bytes 12582916
  165.6 16.6 %copy-start.22 = (bf16[1024,1024]{1,0:T(8,128)(2,1)S(1)}, bf16[1024,1024]{1,0:T(8,128)(2,1)}, u32[]{:S(2)}) copy-start(bf16[1024,1024]{1,0:T(8,128)(2,1)} %param.19) | copy-start | bytes 6291460
  182.3 5.3 copy-start.21
  182.3 6.8 copy-start.39
  185.7 6.4 copy-start.10
  199.7 5.9 copy-start.25
  209.6 5.9 copy-start.24
  237.1 5.4 copy-start.30
  267.3 5.3 copy-start.1
  282.7 7.8 %copy-start.5 = (bf16[8,128,16,64]{1,3,2,0:T(8,128)(2,1)S(1)}, bf16[8,128,16,64]{1,3,2,0:T(8,128)(2,1)}, u32[]{:S(2)}) copy-start(bf16[8,128,16,64]{1,3,2,0:T(8,128)(2,1)} %copy.93) | copy-start | bytes 6291460
  303.0 7.8 %copy-start.35 = (bf16[1024,1024]{1,0:T(8,128)(2,1)S(1)}, bf16[1024,1024]{1,0:T(8,128)(2,1)}, u32[]{:S(2)}) copy-start(bf16[1024,1024]{1,0:T(8,128)(2,1)} %get-tuple-element.45) | copy-start | bytes 6291460
  310.8 6.8 copy-start.17
  310.8 6.8 copy-start.32
  310.8 6.8 copy-start.38
  346.5 352.4 %reduce-scatter.5.cloned.1.call-start = ((), (), s32[]{:S(2)}) async-start(), calls=%async_computation.2 | async-start | bytes 17842176 | tf_op jit(solution)/shard_map/reduce_scatter | solution.py:668
  359.1 26.4 %slice-start = ((s8[11534336]{0:T(1024)(128)(4,1)}), s8[3145728]{0:T(1024)(128)(4,1)S(1)}, s32[]{:S(2)}) async-start(s8[11534336]{0:T(1024)(128)(4,1)} %bitcast.89), calls=%async_computation.4 | async-start | bytes 6291456
  371.0 14.5 %slice-start.1 = ((s8[11534336]{0:T(1024)(128)(4,1)}), s8[4194304]{0:T(1024)(128)(4,1)S(1)}, s32[]{:S(2)}) async-start(s8[11534336]{0:T(1024)(128)(4,1)} %bitcast.89), calls=%async_computation.5 | async-start | bytes 8388608
  371.0 14.5 %slice-start.2 = ((s8[11534336]{0:T(1024)(128)(4,1)}), s8[4194304]{0:T(1024)(128)(4,1)S(1)}, s32[]{:S(2)}) async-start(s8[11534336]{0:T(1024)(128)(4,1)} %bitcast.89), calls=%async_computation.6 | async-start | bytes 8388608
  371.0 14.5 %copy-start.6 = (bf16[1024,1024]{1,0:T(8,128)(2,1)S(1)}, bf16[1024,1024]{1,0:T(8,128)(2,1)}, u32[]{:S(2)}) copy-start(bf16[1024,1024]{1,0:T(8,128)(2,1)} %get-tuple-element.54) | copy-start | bytes 6291460
  412.0 4.2 copy-start.36
  508.0 193.7 %copy-start.26 = (bf16[1024,1024]{1,0:T(8,128)(2,1)S(1)}, bf16[1024,1024]{1,0:T(8,128)(2,1)}, u32[]{:S(2)}) copy-start(bf16[1024,1024]{1,0:T(8,128)(2,1)} %get-tuple-element.117) | copy-start | bytes 6291460
  (21 other events, 63.2 us)
Sparse Core Ops, SparseCore 0:
  346.6 153.6 reduce-scatter.6
  506.7 192.0 reduce-scatter.4
